TPU v7x, 256 devices: a whole 4x4x8 slice. The times are simulated.
256 devices in a mesh: row: 32 (over x_lo, z, core), col: 8 (over x_hi, y).
Axes of the slice: x: 4 (x_hi: 2, x_lo: 2; x = x_hi * 2 + x_lo), y: 4, z: 8, core: 2. Of those that a mesh axis runs over, the one named last changes fastest.
Arguments:
- features: bfloat16 [65536, 512], P(('row', 'col')), may hold values from -6 to 6
- weight: bfloat16 [512, 512], replicated, may hold values from -0.25 to 0.25
- out_grad: bfloat16 [65536, 512], P(('row', 'col')), may hold values from -6 to 6
- relu_mask: int32 [65536, 512], P(('row', 'col')), may hold values 0 or 1
- adjacency_tiles: bfloat16 [49152, 128, 128], P(('row', 'col')), may hold values from -0.1875 to 0.1875
- tile_rows: int32 [49152], P(('row', 'col')), may hold values from 0 to 15
- tile_cols: int32 [49152], P(('row', 'col')), may hold values from 0 to 63
- tile_count: int32 [256], P(('row', 'col')), may hold values from 24 to 192, as said below
Outputs:
- input_grad: bfloat16 [65536, 512], P(('row', 'col'))
- weight_grad: float32 [512, 512], replicated
Inputs may be any that keep to these rules, and one draw needn't show every extreme that they name: Only the first tile_count slots of a device are live; some device has all 192 slots live in every draw.
All inputs are finite; a program needn't handle non-finite values. No bound on the sum of `relu_mask` on one device may be relied on, other than what follows from the above.
Results may differ from a plain program's by a relative error of at most 0.0049.
Values may be sent and summed in bfloat16 or wider, within the bound.
No kernel may reach another device: no remote copies, remote signals or barrier semaphores. Data moves between devices by JAX's collectives and lax.ppermute only.
A program may use at most 128 MiB of HBM per device.

v0:
```python
import math
import jax
import jax.numpy as jnp
from jax import lax
from jax.sharding import PartitionSpec as P

GROUP = 8


def sweep(running, tile_set, block_set, col_set, row_set, live_count, group_size, turns):

    def advance(turn_index, carried):
        first_slot = turn_index * group_size
        part_tiles = lax.dynamic_slice_in_dim(tile_set, first_slot, group_size, 0)
        part_cols = lax.dynamic_slice_in_dim(col_set, first_slot, group_size, 0)
        part_rows = lax.dynamic_slice_in_dim(row_set, first_slot, group_size, 0)
        part_blocks = jnp.take(block_set, part_rows, axis=0)
        slot_ids = first_slot + jnp.arange(group_size, dtype=jnp.int32)
        kept = jnp.where(
            (slot_ids < live_count)[:, None, None], part_tiles, jnp.zeros_like(part_tiles)
        )
        terms = jnp.einsum("tij,tif->tjf", kept, part_blocks, preferred_element_type=jnp.float32)
        return carried.at[part_cols].add(terms)

    return lax.fori_loop(0, turns, advance, running)


def shards(
    features, weight, out_grad, relu_mask, adjacency_tiles, tile_rows, tile_cols, tile_count
):
    tile_size = adjacency_tiles.shape[1]
    feature_width = features.shape[1]
    col_slots = lax.axis_size("row") * (features.shape[0] // tile_size)
    masked_grad = out_grad * relu_mask.astype(jnp.bfloat16)
    panel = lax.all_gather(masked_grad, "col", axis=0, tiled=True)
    grad_blocks = panel.reshape(-1, tile_size, feature_width)
    own_count = tile_count[0]
    slot_sets = (adjacency_tiles, grad_blocks, tile_cols, tile_rows, own_count, True)
    running = jnp.zeros((col_slots, tile_size, feature_width), jnp.float32)
    tile_set, block_set, col_set, row_set, live_count, keep_dead = slot_sets
    turns = tile_set.shape[0] // GROUP
    running = sweep(running, tile_set, block_set, col_set, row_set, live_count, GROUP, turns)
    summed = lax.psum_scatter(
        running.reshape(col_slots * tile_size, feature_width),
        "row",
        scatter_dimension=0,
        tiled=True,
    )
    node_grad = summed.astype(jnp.bfloat16)
    input_grad = lax.dot_general(
        node_grad, weight, (((1,), (1,)), ((), ())), preferred_element_type=jnp.float32
    ).astype(jnp.bfloat16)
    partial_weight = lax.dot_general(
        features, node_grad, (((0,), (0,)), ((), ())), preferred_element_type=jnp.float32
    )
    node_total = features.shape[0] * lax.axis_size("row") * lax.axis_size("col")
    weight_grad = lax.psum(partial_weight, ("row", "col")) * (1.0 / math.sqrt(node_total))
    return (input_grad, weight_grad)


def solution(mesh):
    return jax.shard_map(
        shards,
        mesh=mesh,
        in_specs=(
            P(("row", "col"), None),
            P(),
            P(("row", "col"), None),
            P(("row", "col"), None),
            P(("row", "col"), None, None),
            P(("row", "col")),
            P(("row", "col")),
            P(("row", "col")),
        ),
        out_specs=(P(("row", "col"), None), P()),
        check_vma=False,
    )
```

profile of v0, /device:TPU:2, one launch (start us, length us, event | category | flops | bytes accessed | tf_op | source)
XLA Modules:
  0.0 763.1 jit_solution(5273142124928129784)
XLA Ops:
  9.2 62.6 %all-gather.2.cloned.1.call-done = bf16[2048,512]{1,0:T(8,128)(2,1)} async-done(((bf16[256,512]{1,0:T(8,128)(2,1)}), bf16[2048,512]{1,0:T(8,128)(2,1)}) %all-gather.2.cloned.1.call-update) | async-done | bytes 2097168 | tf_op jit(solution)/shard_map/all_gather | solution.py:35
  71.8 7.9 %broadcast_in_dim.55 = f32[64,128,512]{2,1,0:T(8,128)} broadcast(f32[]{:T(128)} %constant.74.clone.1), dimensions={} | broadcast | bytes 16777220 | tf_op jit(solution)/shard_map/broadcast_in_dim | solution.py:39
  79.7 269.1 %while.13 = (s32[]{:T(128)}, f32[64,128,512]{2,1,0:T(8,128)}, s32[192]{0:T(256)S(1)}, s32[]{:T(128)}, bf16[192,128,128]{2,1,0:T(8,128)(2,1)}, /*index=5*/s32[192...) while((s32[]{:T(128)}, f32[64,128,512]{2,1,0:T(8,128)}, ...), condition=%wide.region_2.3_spmd, body=%wide.region_0.2_spmd.sunk | while | flops 135398496 | bytes 12849583 | solution.py:25
  86.6 4.4 scatter_fusion
  97.8 4.4 scatter_fusion
  120.2 4.4 scatter_fusion
  131.5 4.4 scatter_fusion
  142.7 4.4 scatter_fusion
  154.0 4.3 scatter_fusion
  176.3 4.4 scatter_fusion
  198.7 4.3 scatter_fusion
  209.9 4.4 scatter_fusion
  221.2 4.3 scatter_fusion
  232.4 4.4 scatter_fusion
  243.7 4.3 scatter_fusion
  265.9 4.4 scatter_fusion
  277.2 4.3 scatter_fusion
  288.4 4.4 scatter_fusion
  299.7 4.3 scatter_fusion
  322.1 4.3 scatter_fusion
  333.2 4.4 scatter_fusion
  344.5 4.4 scatter_fusion
  348.9 143.5 %reduce-scatter.2.cloned.1.call-done = f32[256,512]{1,0:T(8,128)} async-done(((f32[8192,512]{1,0:T(8,128)}), f32[256,512]{1,0:T(8,128)}) %reduce-scatter.2.cloned.1.call-update) | async-done | bytes 524304 | tf_op jit(solution)/shard_map/reduce_scatter | solution.py:43
  496.9 257.0 %all-reduce.2.cloned.1.call-done = f32[512,512]{0,1:T(8,128)} async-done(((f32[512,512]{0,1:T(8,128)}), f32[512,512]{0,1:T(8,128)}) %all-reduce.2.cloned.1.call-update) | async-done | bytes 1048592 | tf_op jit(solution)/shard_map/psum | solution.py:57
  (192 shorter events, 194.9 us)
Async XLA Ops:
  7.2 487.6 %copy-start = (bf16[512,512]{1,0:T(8,128)(2,1)S(1)}, bf16[512,512]{1,0:T(8,128)(2,1)}, u32[]{:S(2)}) copy-start(bf16[512,512]{1,0:T(8,128)(2,1)} %param.11) | copy-start | bytes 1572868
  7.2 64.7 %all-gather.2.cloned.1.call-start = ((), (), s32[]{:S(2)}) async-start(), calls=%async_computation.1 | async-start | bytes 2359296 | tf_op jit(solution)/shard_map/all_gather | solution.py:35
  9.2 483.2 %reduce-scatter.2.cloned.1.call-start = ((), (), s32[]{:S(2)}) async-start(), calls=%async_computation.2 | async-start | bytes 17301504 | tf_op jit(solution)/shard_map/reduce_scatter | solution.py:43
  71.8 7.9 %copy-start.2 = (s32[192]{0:T(256)S(1)}, s32[192]{0:T(256)}, u32[]{:S(2)}) copy-start(s32[192]{0:T(256)} %param.15) | copy-start | bytes 2308
  71.8 7.9 %copy-start.3 = (s32[192]{0:T(256)S(1)}, s32[192]{0:T(256)}, u32[]{:S(2)}) copy-start(s32[192]{0:T(256)} %param.16) | copy-start | bytes 2308
  348.8 143.6 %copy-start.1 = (bf16[256,512]{1,0:T(8,128)(2,1)S(1)}, bf16[256,512]{1,0:T(8,128)(2,1)}, u32[]{:S(2)}) copy-start(bf16[256,512]{1,0:T(8,128)(2,1)} %param.10) | copy-start | bytes 786436
  348.9 405.0 %all-reduce.2.cloned.1.call-start = ((), (), s32[]{:S(2)}) async-start(), calls=%async_computation.3 | async-start | bytes 2097152 | tf_op jit(solution)/shard_map/psum | solution.py:57
Sparse Core Ops, SparseCore 0:
  11.2 60.5 all-gather.1
  349.0 143.3 reduce-scatter.1
  498.4 255.4 all-reduce.1
where the time goes:
time: 767 us; the launch traced here: 763 us
  waiting for transfers between devices  463 us (60%)
  other arithmetic  127 us (17%)
  local copies, waits for them, and re-layouts  113 us (15%)
  matrix products  45.6 us (6%)
  between operations  13.8 us (2%)
    psum x1, waiting for transfers between devices, shards(): lax.psum(partial_weight, ('row', 'col')) * (1.0 / math.sqrt(node_total))  257 us
    reduce_scatter x1, waiting for transfers between devices, shards(): lax.psum_scatter(running.reshape(col_slots * tile_size, feature_width), '...  143 us
    scatter-add x24, other arithmetic, advance(): return carried.at[part_cols].add(terms)  104 us
    gather x24, local copies, waits for them, and re-layouts, advance(): part_blocks = jnp.take(block_set, part_rows, axis=0)  76.2 us
    all_gather x1, waiting for transfers between devices, shards(): panel = lax.all_gather(masked_grad, 'col', axis=0, tiled=True)  62.6 us
    dot_general x24, matrix products, advance(): jnp.einsum('tij,tif->tjf', kept, part_blocks, preferred_element_type=jnp....  41.1 us
    dynamic_slice x48, local copies, waits for them, and re-layouts, advance(): part_tiles = lax.dynamic_slice_in_dim(tile_set, first_slot, group_size, 0)  27.7 us
    and x24, other arithmetic, advance(): part_blocks = jnp.take(block_set, part_rows, axis=0)  17.4 us
  transfers between devices with their start and end apart: 3, of which 3 were waited for; matrix products, arithmetic and copies ran while one was open for 0% of the time, Pallas kernels for 0%

commit v1 on v0

--- a/solution.py
+++ b/solution.py
@@ -32,7 +32,9 @@
     feature_width = features.shape[1]
     col_slots = lax.axis_size("row") * (features.shape[0] // tile_size)
     masked_grad = out_grad * relu_mask.astype(jnp.bfloat16)
-    panel = lax.all_gather(masked_grad, "col", axis=0, tiled=True)
+    panel = jnp.concatenate(
+        lax.all_to_all(jnp.stack([masked_grad] * lax.axis_size("col")), "col", 0, 0), axis=0
+    )
     grad_blocks = panel.reshape(-1, tile_size, feature_width)
     own_count = tile_count[0]
     slot_sets = (adjacency_tiles, grad_blocks, tile_cols, tile_rows, own_count, True)

time: 767 us -> 740 us (0.965)
  waiting for transfers between devices: 463 us -> 430 us
    all_gather x1 -> x0, waiting for transfers between devices: 62.6 us -> none  [shards(): panel = lax.all_gather(masked_grad, 'col', axis=0, tiled=True)]
    all_to_all x0 -> x1, waiting for transfers between devices: none -> 26.5 us  [shards(): lax.all_to_all(jnp.stack([masked_grad] * lax.axis_size('col')), 'col', 0, 0)]
where the time goes in v1:
time: 740 us; the launch traced here: 737 us
  waiting for transfers between devices  430 us (58%)
  other arithmetic  126 us (17%)
  local copies, waits for them, and re-layouts  115 us (16%)
  matrix products  45.6 us (6%)
  between operations  14.1 us (2%)
    psum x1, waiting for transfers between devices, shards(): lax.psum(partial_weight, ('row', 'col')) * (1.0 / math.sqrt(node_total))  257 us
    reduce_scatter x1, waiting for transfers between devices, shards(): lax.psum_scatter(running.reshape(col_slots * tile_size, feature_width), '...  146 us
    scatter-add x24, other arithmetic, advance(): return carried.at[part_cols].add(terms)  104 us
    gather x24, local copies, waits for them, and re-layouts, advance(): part_blocks = jnp.take(block_set, part_rows, axis=0)  76.2 us
    dot_general x24, matrix products, advance(): jnp.einsum('tij,tif->tjf', kept, part_blocks, preferred_element_type=jnp....  41.1 us
    dynamic_slice x48, local copies, waits for them, and re-layouts, advance(): part_tiles = lax.dynamic_slice_in_dim(tile_set, first_slot, group_size, 0)  27.7 us
    all_to_all x1, waiting for transfers between devices, shards(): lax.all_to_all(jnp.stack([masked_grad] * lax.axis_size('col')), 'col', 0, 0)  26.5 us
    and x24, other arithmetic, advance(): part_blocks = jnp.take(block_set, part_rows, axis=0)  17.4 us
  transfers between devices with their start and end apart: 3, of which 3 were waited for; matrix products, arithmetic and copies ran while one was open for 0% of the time, Pallas kernels for 0%

profile of v1, /device:TPU:2, one launch (start us, length us, event | category | flops | bytes accessed | tf_op | source)
XLA Modules:
  0.0 736.5 jit_solution(4451299421205433960)
XLA Ops:
  9.9 6.0 all-to-all-start
  16.0 26.5 %all-to-all-done = bf16[8,256,512]{2,1,0:T(8,128)(2,1)} async-done(((bf16[8,256,512]{2,1,0:T(8,128)(2,1)}), bf16[8,256,512]{2,1,0:T(8,128)(2,1)}, u32[]{:S(2)}, u32[]{:S(2)}) %all-to-all-start) | async-done | bytes 2097184 | tf_op jit(solution)/shard_map/all_to_all | solution.py:36
  42.5 7.9 %broadcast_in_dim.55 = f32[64,128,512]{2,1,0:T(8,128)} broadcast(f32[]{:T(128)} %constant.74.clone.1), dimensions={} | broadcast | bytes 16777220 | tf_op jit(solution)/shard_map/broadcast_in_dim | solution.py:41
  50.4 269.0 %while.13 = (s32[]{:T(128)}, f32[64,128,512]{2,1,0:T(8,128)}, s32[192]{0:T(256)S(1)}, s32[]{:T(128)}, bf16[192,128,128]{2,1,0:T(8,128)(2,1)}, /*index=5*/s32[192...) while((s32[]{:T(128)}, f32[64,128,512]{2,1,0:T(8,128)}, ...), condition=%wide.region_2.3_spmd, body=%wide.region_0.2_spmd.sunk | while | flops 135398496 | bytes 12849583 | solution.py:25
  57.2 4.4 scatter_fusion
  68.5 4.4 scatter_fusion
  79.7 4.3 scatter_fusion
  90.9 4.4 scatter_fusion
  102.2 4.4 scatter_fusion
  113.4 4.4 scatter_fusion
  147.0 4.4 scatter_fusion
  180.5 4.4 scatter_fusion
  191.7 4.3 scatter_fusion
  202.9 4.4 scatter_fusion
  225.3 4.3 scatter_fusion
  236.5 4.4 scatter_fusion
  247.8 4.4 scatter_fusion
  259.0 4.4 scatter_fusion
  270.3 4.3 scatter_fusion
  292.6 4.3 scatter_fusion
  303.8 4.4 scatter_fusion
  315.0 4.3 scatter_fusion
  319.4 146.1 %reduce-scatter.2.cloned.1.call-done = f32[256,512]{1,0:T(8,128)} async-done(((f32[8192,512]{1,0:T(8,128)}), f32[256,512]{1,0:T(8,128)}) %reduce-scatter.2.cloned.1.call-update) | async-done | bytes 524304 | tf_op jit(solution)/shard_map/reduce_scatter | solution.py:45
  470.0 257.1 %all-reduce.2.cloned.1.call-done = f32[512,512]{0,1:T(8,128)} async-done(((f32[512,512]{0,1:T(8,128)}), f32[512,512]{0,1:T(8,128)}) %all-reduce.2.cloned.1.call-update) | async-done | bytes 1048592 | tf_op jit(solution)/shard_map/psum | solution.py:59
  (192 shorter events, 199.9 us)
Async XLA Ops:
  7.2 460.7 %copy-start = (bf16[512,512]{1,0:T(8,128)(2,1)S(1)}, bf16[512,512]{1,0:T(8,128)(2,1)}, u32[]{:S(2)}) copy-start(bf16[512,512]{1,0:T(8,128)(2,1)} %param.11) | copy-start | bytes 1572868
  9.9 32.6 %all-to-all-start = ((bf16[8,256,512]{2,1,0:T(8,128)(2,1)}), bf16[8,256,512]{2,1,0:T(8,128)(2,1)}, u32[]{:S(2)}, u32[]{:S(2)}) async-start(bf16[8,256,512]{2,1,0:T(8,128)(2,1)} %stack.2), calls=%async_computation | async-start | bytes 4194304 | tf_op jit(solution)/shard_map/all_to_all | solution.py:36
  16.0 449.6 %reduce-scatter.2.cloned.1.call-start = ((), (), s32[]{:S(2)}) async-start(), calls=%async_computation.2 | async-start | bytes 17301504 | tf_op jit(solution)/shard_map/reduce_scatter | solution.py:45
  42.5 7.9 %copy-start.2 = (s32[192]{0:T(256)S(1)}, s32[192]{0:T(256)}, u32[]{:S(2)}) copy-start(s32[192]{0:T(256)} %param.15) | copy-start | bytes 2308
  42.5 7.9 %copy-start.3 = (s32[192]{0:T(256)S(1)}, s32[192]{0:T(256)}, u32[]{:S(2)}) copy-start(s32[192]{0:T(256)} %param.16) | copy-start | bytes 2308
  319.3 146.2 %copy-start.1 = (bf16[256,512]{1,0:T(8,128)(2,1)S(1)}, bf16[256,512]{1,0:T(8,128)(2,1)}, u32[]{:S(2)}) copy-start(bf16[256,512]{1,0:T(8,128)(2,1)} %param.10) | copy-start | bytes 786436
  319.4 407.7 %all-reduce.2.cloned.1.call-start = ((), (), s32[]{:S(2)}) async-start(), calls=%async_computation.3 | async-start | bytes 2097152 | tf_op jit(solution)/shard_map/psum | solution.py:59
Sparse Core Ops, SparseCore 0:
  319.5 146.0 reduce-scatter.1
  471.6 255.4 all-reduce.1
